TPU v7x, 32 devices: a whole 2x2x4 slice. The times are simulated.
32 devices in a mesh: aux: 4 (over y, x), blk: 8 (over z, core).
Axes of the slice: x: 2, y: 2, z: 4, core: 2. Of those that a mesh axis runs over, the one named last changes fastest.
Arguments:
- three_center: bfloat16 [384, 4, 128, 128], P(('aux', 'blk')), may hold values from -6 to 6
- slot_block: int32 [384], P(('aux', 'blk')), may hold values from 0 to 47
- slot_aux: int32 [384], P(('aux', 'blk')), may hold values from 0 to 1
- live_slots: int32 [32], P(('aux', 'blk')), may hold values from 1 to 12, as said below
- vir_coef: bfloat16 [6144, 256], replicated, may hold values from -0.00478416 to 0.00478416
- eps_occ: float32 [4000], replicated, may hold values from -1.5 to -0.3
- eps_vir: float32 [256], replicated, may hold values from 0.2 to 3
- occ_index: int32 [4], replicated, may hold values from 0 to 3999, as said below
Outputs:
- amplitudes: float32 [4, 256, 4, 256], P('aux', 'blk')
- pair_energy: float32 [4, 4], P('aux')
Inputs may be any that keep to these rules, and one draw needn't show every extreme that they name: The slots in use on a device are its first live_slots ones; the others hold data that is not used. Some device holds exactly 12 slots in use in every draw. `occ_index`: the indices are distinct; the first and the last occupied orbital of the system are in every batch.
All inputs are finite; a program needn't handle non-finite values.
Results may differ from a plain program's by a relative error of at most 0.0035.
Values may be sent and summed in bfloat16 or wider, within the bound.
A program may use at most 64 MiB of HBM per device.

v0:
```python
import jax
import jax.numpy as jnp
from jax import lax
from jax.sharding import PartitionSpec as P

AUX_BLOCKS_DEV = 2


def body(three_center, slot_block, slot_aux, live_slots, vir_coef, eps_occ, eps_vir, occ_index):
    blk_count = lax.axis_size("blk")
    occ_row = lax.axis_index("aux")
    slot_count = three_center.shape[0]
    occ_count = three_center.shape[1]
    ao_span = three_center.shape[3]
    vir_count = vir_coef.shape[1]
    coef_blocks = vir_coef.reshape(vir_coef.shape[0] // ao_span, ao_span, vir_count)
    coefficients = jnp.take(coef_blocks, slot_block, axis=0)
    products = jnp.einsum(
        "soqn,snv->soqv", three_center, coefficients, preferred_element_type=jnp.float32
    )
    keep = (jnp.arange(slot_count) < live_slots[0]).astype(jnp.float32)
    select = (slot_aux[:, None] == jnp.arange(AUX_BLOCKS_DEV)[None, :]).astype(jnp.float32)
    select = select * keep[:, None]
    local_rows = jnp.einsum("sk,soqv->kqov", select, products).astype(jnp.bfloat16)
    halfed = lax.all_gather(local_rows, "aux", axis=0, tiled=True)
    own_rows = lax.dynamic_index_in_dim(halfed, occ_row, 2, keepdims=False)
    rows_dev = vir_count // blk_count
    mixed = lax.dot_general(
        halfed, own_rows, (((0, 1), (0, 1)), ((), ())), preferred_element_type=jnp.float32
    )
    summed = lax.psum_scatter(
        jnp.stack(
            [
                lax.dot_general(
                    own_rows,
                    halfed,
                    (((0, 1), (0, 1)), ((), ())),
                    preferred_element_type=jnp.float32,
                ),
                jnp.transpose(mixed, (1, 0, 2)),
            ],
            axis=1,
        ),
        "blk",
        scatter_dimension=0,
        tiled=True,
    )
    direct = summed[:, 0]
    crossed = summed[:, 1]
    first_vir = lax.axis_index("blk") * rows_dev
    occ_levels = jnp.take(eps_occ, occ_index)
    own_level = jnp.sum(jnp.where(jnp.arange(occ_count) == occ_row, occ_levels, 0.0))
    vir_levels = lax.dynamic_slice_in_dim(eps_vir, first_vir, rows_dev, 0)
    denominator = (
        own_level + occ_levels[None, :, None] - vir_levels[:, None, None] - eps_vir[None, None, :]
    )
    amplitudes = (direct / denominator)[None]
    pair_part = jnp.sum(direct * (2.0 * direct - crossed) / denominator, axis=(0, 2))
    pair_energy = lax.psum(pair_part, "blk")[None]
    return (amplitudes, pair_energy)


def solution(mesh):
    in_specs = (
        P(("aux", "blk"), None, None, None),
        P(("aux", "blk")),
        P(("aux", "blk")),
        P(("aux", "blk")),
        P(),
        P(),
        P(),
        P(),
    )
    out_specs = (P("aux", "blk", None, None), P("aux", None))
    return jax.shard_map(body, mesh=mesh, in_specs=in_specs, out_specs=out_specs, check_vma=False)
```

profile of v0, /device:TPU:0, one launch (start us, length us, event | category | flops | bytes accessed | tf_op | source)
XLA Modules:
  0.0 131.5 jit_solution(10336060481008152967)
XLA Ops:
  7.2 0.0 copy-start
  7.2 0.0 all-gather.2.cloned.1.call-start
  7.2 0.8 compare_select_fusion.1
  8.0 0.8 compare_and_fusion
  8.8 0.3 copy-done
  9.1 1.5 %gather_fusion = bf16[12,128,256]{2,1,0:T(8,128)(2,1)} fusion(bf16[48,128,256]{2,1,0:T(8,128)(2,1)S(1)} %bitcast.68, s32[1024]{0:T(1024)S(1)} %pad_clamp_fusion.1), kind=kCustom, calls=%fused_computation | custom fusion | bytes 1572912 | tf_op jit(solution)/shard_map/jit(_take)/gather | solution.py:17
  10.6 4.8 %convolution_bitcast_fusion = bf16[12,4,128,256]{2,3,1,0:T(8,128)(2,1)} fusion(bf16[12,4,128,128]{3,2,1,0:T(8,128)(2,1)} %param.8, bf16[12,128,256]{2,1,0:T(8,128)(2,1)} %gather_fusion, pred[12]{0:T(512)(128)(4,1)S(1)} %compare_and_fusion), kind=kOutput, calls=%fused_computation.2 | convolution fusion | flops 403046400 | bytes 5505036 | tf_op jit(solution)/shard_map/soqn,snv->soqv/dot_general | solution.py:18
  15.4 7.7 %copy.28 = bf16[12,4,128,256]{3,0,2,1:T(8,128)(2,1)} copy(bf16[12,4,128,256]{2,3,1,0:T(8,128)(2,1)} %convolution_bitcast_fusion) | data formatting | bytes 6291456 | tf_op jit(solution)/shard_map/soqn,snv->soqv/dot_general | solution.py:18
  23.7 0.0 copy-done.4
  23.7 2.9 %fusion = bf16[2,128,4,256]{3,0,1,2:T(2,128)(2,1)S(1)} fusion(bf16[12,4,128,256]{3,0,2,1:T(8,128)(2,1)} %copy.28, bf16[12]{0:T(256)(128)(2,1)S(1)} %compare_convert_fusion, s32[12]{0:T(128)S(1)} %copy-done.4), kind=kOutput, calls=%fused_computation.7 | convolution fusion | flops 6291504 | bytes 3670088 | tf_op jit(solution)/shard_map/sk,soqv->kqov/dot_general | solution.py:24
  26.6 0.9 copy.29
  27.5 0.0 all-gather.2.cloned.1.call-update
  27.5 0.0 reduce-scatter.2.cloned.1.call-start
  27.6 38.0 %all-gather.2.cloned.1.call-done = bf16[8,128,4,256]{3,1,2,0:T(8,128)(2,1)} async-done(((bf16[2,128,4,256]{3,1,2,0:T(8,128)(2,1)}), bf16[8,128,4,256]{3,1,2,0:T(8,128)(2,1)}) %all-gather.2.cloned.1.call-update) | async-done | bytes 2097168 | tf_op jit(solution)/shard_map/all_gather | solution.py:25
  65.6 2.6 %convolution_bitcast_fusion.2 = f32[256,1,4,256]{3,0,2,1:T(8,128)S(1)} fusion(bf16[8,128,4,256]{3,1,2,0:T(8,128)(2,1)} %all-gather.2.cloned.1.call-done, s32[]{:T(128)S(6)} %select_n.33), kind=kOutput, calls=%fused_computation.5 | convolution fusion | flops 536870912 | bytes 3670020 | tf_op jit(solution)/shard_map/dot_general | solution.py:28
  68.2 0.0 copy-done.5
  68.2 0.7 convolution_bitcast_fusion.1
  68.9 1.5 %pad_maximum_fusion = f32[256,2,4,256]{3,0,2,1:T(8,128)} fusion(f32[256,1,4,256]{3,0,2,1:T(8,128)S(1)} %convolution_bitcast_fusion.2, f32[256,1,4,256]{3,0,2,1:T(8,128)S(1)} %convolution_bitcast_fusion.1), kind=kLoop, calls=%fused_computation.3 | loop fusion | flops 524288 | bytes 4194304 | tf_op jit(solution)/shard_map/stack | solution.py:32
  70.4 0.0 reduce-scatter.2.cloned.1.call-update
  70.4 0.6 copy-done.2
  71.1 0.1 dynamic_slice.8
  71.2 0.0 copy-done.3
  71.2 0.0 copy-done.1
  71.2 0.6 gather_fusion.1
  71.8 0.6 fusion.16
  72.4 0.7 broadcast_add_fusion
  73.1 0.1 broadcast_subtract_fusion
  73.2 33.5 %reduce-scatter.2.cloned.1.call-done = f32[32,2,4,256]{3,0,2,1:T(8,128)} async-done(((f32[256,2,4,256]{3,0,2,1:T(8,128)}), f32[32,2,4,256]{3,0,2,1:T(8,128)}) %reduce-scatter.2.cloned.1.call-update) | async-done | bytes 262160 | tf_op jit(solution)/shard_map/reduce_scatter | solution.py:31
  106.7 1.0 bitcast_divide_fusion
  107.7 0.7 copy.34
  108.4 1.2 fusion.12
  109.6 15.1 %psum.7 = f32[1,4]{1,0:T(1,128)} all-reduce(f32[1,4]{1,0:T(1,128)S(1)} %bitcast.69), channel_id=1, replica_groups=mesh['aux'=4,'blk'=8] {'blk'}, use_global_device_ids=true, to_apply=%region_3.4 | all-reduce | flops 4 | bytes 32 | tf_op jit(solution)/shard_map/psum | solution.py:59
  (9 shorter events, 0.0 us)
Async XLA Ops:
  7.2 1.9 %copy-start = (bf16[6144,256]{1,0:T(8,128)(2,1)S(1)}, bf16[6144,256]{1,0:T(8,128)(2,1)}, u32[]{:S(2)}) copy-start(bf16[6144,256]{1,0:T(8,128)(2,1)} %param.12) | copy-start | bytes 9437188
  7.2 58.4 %all-gather.2.cloned.1.call-start = ((), (), s32[]{:S(2)}) async-start(), calls=%async_computation.1 | async-start | bytes 2621440 | tf_op jit(solution)/shard_map/all_gather | solution.py:25
  15.4 8.4 %copy-start.4 = (s32[12]{0:T(128)S(1)}, s32[12]{0:T(128)}, u32[]{:S(2)}) copy-start(s32[12]{0:T(128)} %param.10) | copy-start | bytes 148
  27.5 79.1 %reduce-scatter.2.cloned.1.call-start = ((), (), s32[]{:S(2)}) async-start(), calls=%async_computation.2 | async-start | bytes 2359296 | tf_op jit(solution)/shard_map/reduce_scatter | solution.py:31
  65.6 2.6 %copy-start.5 = (bf16[8,128,4,256]{3,1,2,0:T(8,128)(2,1)S(1)}, bf16[8,128,4,256]{3,1,2,0:T(8,128)(2,1)}, u32[]{:S(2)}) copy-start(bf16[8,128,4,256]{3,1,2,0:T(8,128)(2,1)} %all-gather.2.cloned.1.call-done) | copy-start | bytes 6291460
  70.4 0.7 copy-start.2
  70.4 0.8 copy-start.3
  70.4 0.8 copy-start.1
Sparse Core Ops, SparseCore 0:
  27.6 37.8 all-gather.1
  70.6 36.0 reduce-scatter.1
where the time goes:
time: 132 us; the launch traced here: 131 us
  waiting for transfers between devices  71.6 us (54%)
  blocking collectives  15.1 us (11%)
  between operations  14.8 us (11%)
  local copies, waits for them, and re-layouts  12.5 us (9%)
  matrix products  11 us (8%)
  other arithmetic  6.57 us (5%)
    all_gather x1, waiting for transfers between devices, body(): halfed = lax.all_gather(local_rows, 'aux', axis=0, tiled=True)  38 us
    reduce_scatter x1, waiting for transfers between devices, body(): lax.psum_scatter(jnp.stack([lax.dot_general(own_rows, halfed, (((0, 1), (...  33.5 us
    psum x1, blocking collectives, body(): pair_energy = lax.psum(pair_part, 'blk')[None]  15.1 us
    dot_general x1, local copies, waits for them, and re-layouts, body(): jnp.einsum('soqn,snv->soqv', three_center, coefficients, preferred_elemen...  7.69 us
    dot_general x1, matrix products, body(): jnp.einsum('soqn,snv->soqv', three_center, coefficients, preferred_elemen...  4.8 us
    dot_general x1, matrix products, body(): jnp.einsum('sk,soqv->kqov', select, products).astype(jnp.bfloat16)  2.88 us
  transfers between devices with their start and end apart: 2, of which 2 were waited for; matrix products, arithmetic and copies ran while one was open for 2% of the time, Pallas kernels for 0%

commit v1 on v0

--- a/solution.py
+++ b/solution.py
@@ -7,6 +7,21 @@
 
 
 def body(three_center, slot_block, slot_aux, live_slots, vir_coef, eps_occ, eps_vir, occ_index):
+
+    def change_stocks(mat, which_axis):
+        shares = jax.lax.axis_size(which_axis)
+        near = range(shares)
+        all_values = map(lambda t: (t, (t + 1) % shares), near)
+        views = list(all_values)
+        block_next = [None] * shares
+        block_next[shares - 1] = mat
+        for no in range(shares - 2, -1, -1):
+            block_next[no] = jax.lax.ppermute(block_next[no + 1], axis_name=which_axis, perm=views)
+        r_now = jnp.concatenate(block_next, axis=0)
+        outer = jax.lax.axis_index(which_axis)
+        oldest = (outer + 1) * mat.shape[0]
+        return jnp.roll(r_now, oldest, axis=0)
+
     blk_count = lax.axis_size("blk")
     occ_row = lax.axis_index("aux")
     slot_count = three_center.shape[0]
@@ -22,7 +37,7 @@
     select = (slot_aux[:, None] == jnp.arange(AUX_BLOCKS_DEV)[None, :]).astype(jnp.float32)
     select = select * keep[:, None]
     local_rows = jnp.einsum("sk,soqv->kqov", select, products).astype(jnp.bfloat16)
-    halfed = lax.all_gather(local_rows, "aux", axis=0, tiled=True)
+    halfed = change_stocks(local_rows, "aux")
     own_rows = lax.dynamic_index_in_dim(halfed, occ_row, 2, keepdims=False)
     rows_dev = vir_count // blk_count
     mixed = lax.dot_general(

time: 132 us -> 164 us (1.24); the launches traced: 131 us -> 162 us
  local copies, waits for them, and re-layouts: 12.5 us -> 38.6 us
  starting transfers between devices: 0.08 us -> 3.8 us
    ppermute x0 -> x3, waiting for transfers between devices: none -> 39.6 us  [change_stocks(): jax.lax.ppermute(block_next[no + 1], axis_name=which_axis, perm=views)]
    all_gather x1 -> x0, waiting for transfers between devices: 38 us -> none  [body(): halfed = lax.all_gather(local_rows, 'aux', axis=0, tiled=True)]
    concatenate x0 -> x1, local copies, waits for them, and re-layouts: none -> 20 us  [change_stocks(): return jnp.roll(r_now, oldest, axis=0)]
    dynamic_slice x0 -> x3, local copies, waits for them, and re-layouts: none -> 4.34 us  [the longest x1 2.84 us: change_stocks(): return jnp.roll(r_now, oldest, axis=0)]
    ppermute x0 -> x3, starting transfers between devices: none -> 3.76 us  [change_stocks(): jax.lax.ppermute(block_next[no + 1], axis_name=which_axis, perm=views)]
  transfers between devices with their start and end apart: 2 -> 4, of which waited for: 2 -> 4; matrix products, arithmetic and copies ran while one was open for 2% -> 1% of each run, Pallas kernels for 0% -> 0%
where the time goes in v1:
time: 164 us; the launch traced here: 162 us
  waiting for transfers between devices  72.9 us (44%)
  local copies, waits for them, and re-layouts  38.6 us (24%)
  blocking collectives  15.4 us (9%)
  between operations  14.8 us (9%)
  matrix products  9.58 us (6%)
  other arithmetic  6.56 us (4%)
  starting transfers between devices  3.8 us (2%)
    ppermute x3, waiting for transfers between devices, change_stocks(): jax.lax.ppermute(block_next[no + 1], axis_name=which_axis, perm=views)  39.6 us
    reduce_scatter x1, waiting for transfers between devices, body(): lax.psum_scatter(jnp.stack([lax.dot_general(own_rows, halfed, (((0, 1), (...  33.2 us
    concatenate x1, local copies, waits for them, and re-layouts, change_stocks(): return jnp.roll(r_now, oldest, axis=0)  20 us
    psum x1, blocking collectives, body(): pair_energy = lax.psum(pair_part, 'blk')[None]  15.4 us
    dot_general x1, local copies, waits for them, and re-layouts, body(): jnp.einsum('soqn,snv->soqv', three_center, coefficients, preferred_elemen...  7.71 us
    dot_general x1, matrix products, body(): jnp.einsum('soqn,snv->soqv', three_center, coefficients, preferred_elemen...  4.81 us
    ppermute x3, starting transfers between devices, change_stocks(): jax.lax.ppermute(block_next[no + 1], axis_name=which_axis, perm=views)  3.76 us
  transfers between devices with their start and end apart: 4, of which 4 were waited for; matrix products, arithmetic and copies ran while one was open for 1% of the time, Pallas kernels for 0%

profile of v1, /device:TPU:0, one launch (start us, length us, event | category | flops | bytes accessed | tf_op | source)
XLA Modules:
  0.0 161.6 jit_solution(11357698906469877163)
XLA Ops:
  7.2 0.8 compare_and_fusion
  8.0 0.8 compare_select_fusion.1
  9.5 1.5 gather_fusion
  11.0 4.8 %fusion.13 = bf16[12,256,4,128]{3,1,2,0:T(8,128)(2,1)} fusion(bf16[12,4,128,128]{3,2,1,0:T(8,128)(2,1)} %param.8, bf16[12,128,256]{2,1,0:T(8,128)(2,1)} %gather_fusion, pred[12]{0:T(512)(128)(4,1)S(1)} %compare_and_fusion), kind=kOutput, calls=%fused_computation.11 | convolution fusion | flops 403046400 | bytes 5505036 | tf_op jit(solution)/shard_map/soqn,snv->soqv/dot_general | solution.py:33
  15.8 7.7 %copy.20 = bf16[12,256,4,128]{1,0,3,2:T(8,128)(2,1)} copy(bf16[12,256,4,128]{3,1,2,0:T(8,128)(2,1)} %fusion.13) | data formatting | bytes 6291456 | tf_op jit(solution)/shard_map/soqn,snv->soqv/dot_general | solution.py:33
  23.5 2.9 %fusion.10 = bf16[2,128,4,256]{3,0,1,2:T(2,128)(2,1)S(1)} fusion(bf16[12,256,4,128]{1,0,3,2:T(8,128)(2,1)} %copy.20, bf16[12]{0:T(256)(128)(2,1)S(1)} %compare_convert_fusion, s32[12]{0:T(128)S(1)} %copy-done.6), kind=kOutput, calls=%fused_computation.10 | convolution fusion | flops 6291504 | bytes 3670088 | tf_op jit(solution)/shard_map/sk,soqv->kqov/dot_general | solution.py:39
  26.4 0.8 copy-done.2
  27.2 3.0 %collective-permute-start = (bf16[2,128,4,256]{3,0,1,2:T(2,128)(2,1)S(1)}, bf16[2,128,4,256]{3,0,1,2:T(2,128)(2,1)S(1)}, u32[]{:S(2)}, u32[]{:S(2)}) collective-permute-start(bf16[2,128,4,256]{3,0,1,2:T(2,128)(2,1)S(1)} %fusion.10), channel_id=1, source_target_pairs={{0,8},{8,16},{16,24},{24,0},{1,9},{9,17},{17,25},{25,1},{2,10},{10... | collective-permute-start | bytes 1572872 | tf_op jit(solution)/shard_map/ppermute | solution.py:19
  30.2 12.9 %collective-permute-done = bf16[2,128,4,256]{3,0,1,2:T(2,128)(2,1)S(1)} collective-permute-done((bf16[2,128,4,256]{3,0,1,2:T(2,128)(2,1)S(1)}, bf16[2,128,4,256]{3,0,1,2:T(2,128)(2,1)S(1)}, u32[]{:S(2)}, u32[]{:S(2)}) %collective-permute-start) | collective-permute-done | bytes 524320 | tf_op jit(solution)/shard_map/ppermute | solution.py:19
  43.0 0.8 copy-done.3
  43.8 0.8 collective-permute-start.1
  44.6 13.3 %collective-permute-done.1 = bf16[2,128,4,256]{3,0,1,2:T(2,128)(2,1)} collective-permute-done((bf16[2,128,4,256]{3,0,1,2:T(2,128)(2,1)S(1)}, bf16[2,128,4,256]{3,0,1,2:T(2,128)(2,1)}, u32[]{:S(2)}, u32[]{:S(2)}) %collective-permute-start.1) | collective-permute-done | bytes 524320 | tf_op jit(solution)/shard_map/ppermute | solution.py:19
  57.9 13.4 %collective-permute-done.2 = bf16[2,128,4,256]{3,0,1,2:T(2,128)(2,1)} collective-permute-done((bf16[2,128,4,256]{3,0,1,2:T(2,128)(2,1)}, bf16[2,128,4,256]{3,0,1,2:T(2,128)(2,1)}, u32[]{:S(2)}, u32[]{:S(2)}) %collective-permute-start.2) | collective-permute-done | bytes 524320 | tf_op jit(solution)/shard_map/ppermute | solution.py:19
  71.4 20.0 %concatenate.6 = bf16[16,128,4,256]{3,0,1,2:T(8,128)(2,1)} concatenate(bf16[2,128,4,256]{3,0,1,2:T(2,128)(2,1)} %collective-permute-done.2, bf16[2,128,4,256]{3,0,1,2:T(2,128)(2,1)} %collective-permute-done.1, bf16[2,128,4,256]{3,0,1,2:T(2,128)(2,1)} %copy-done.3, bf16[2,128,4,256]{3,0,1,2:T(2,128)(2,1)} %copy-done.2, bf16[2,128,4,256]{3,0,1,2:T(2,128)(2,1)} %collective-permute-done.2, ...), dimensions={0} | concatenate | bytes 8388608 | tf_op jit(solution)/shard_map/jit(_roll_dynamic)/concatenate | solution.py:23
  91.4 1.4 fusion.35
  92.7 1.4 constant_dynamic-slice_fusion.1
  94.1 2.8 %constant_dynamic-slice_fusion = bf16[8,128,4,256]{3,0,1,2:T(8,128)(2,1)S(1)} fusion(bf16[16,128,4,256]{3,0,1,2:T(8,128)(2,1)} %concatenate.6, s32[]{:T(128)S(6)} %select_n.51), kind=kLoop, calls=%fused_computation.42 | loop fusion | bytes 4194308 | tf_op jit(solution)/shard_map/jit(_roll_dynamic)/dynamic_slice | solution.py:23
  97.0 0.1 copy.39
  97.1 1.1 convolution_bitcast_fusion
  98.2 0.8 fusion.4
  99.0 1.5 pad_maximum_fusion
  100.5 0.6 copy-done.4
  101.2 0.1 dynamic_slice.14
  101.3 0.6 gather_fusion.1
  101.9 0.6 fusion.27
  102.5 0.7 broadcast_add_fusion
  103.2 0.1 broadcast_subtract_fusion
  103.2 33.2 %reduce-scatter.2.cloned.1.call-done = f32[32,2,4,256]{3,0,2,1:T(8,128)} async-done(((f32[256,2,4,256]{3,0,2,1:T(8,128)}), f32[32,2,4,256]{3,0,2,1:T(8,128)}) %reduce-scatter.2.cloned.1.call-update) | async-done | bytes 262160 | tf_op jit(solution)/shard_map/reduce_scatter | solution.py:46
  136.5 1.0 bitcast_divide_fusion
  137.5 0.7 copy.18
  138.2 1.2 fusion.23
  139.4 15.4 %psum.7 = f32[1,4]{1,0:T(1,128)} all-reduce(f32[1,4]{1,0:T(1,128)S(1)} %bitcast.65), channel_id=1, replica_groups=mesh['aux'=4,'blk'=8] {'blk'}, use_global_device_ids=true, to_apply=%region_3.4 | all-reduce | flops 4 | bytes 32 | tf_op jit(solution)/shard_map/psum | solution.py:74
  (18 shorter events, 0.1 us)
Async XLA Ops:
  7.2 2.3 %copy-start = (bf16[6144,256]{1,0:T(8,128)(2,1)S(1)}, bf16[6144,256]{1,0:T(8,128)(2,1)}, u32[]{:S(2)}) copy-start(bf16[6144,256]{1,0:T(8,128)(2,1)} %param.12) | copy-start | bytes 9437188
  7.2 129.3 %reduce-scatter.2.cloned.1.call-start = ((), (), s32[]{:S(2)}) async-start(), calls=%async_computation.1 | async-start | bytes 2359296 | tf_op jit(solution)/shard_map/reduce_scatter | solution.py:46
  15.8 7.7 %copy-start.6 = (s32[12]{0:T(128)S(1)}, s32[12]{0:T(128)}, u32[]{:S(2)}) copy-start(s32[12]{0:T(128)} %param.10) | copy-start | bytes 148
  26.4 0.8 copy-start.2
  27.2 15.8 %collective-permute-start = (bf16[2,128,4,256]{3,0,1,2:T(2,128)(2,1)S(1)}, bf16[2,128,4,256]{3,0,1,2:T(2,128)(2,1)S(1)}, u32[]{:S(2)}, u32[]{:S(2)}) collective-permute-start(bf16[2,128,4,256]{3,0,1,2:T(2,128)(2,1)S(1)} %fusion.10), channel_id=1, source_target_pairs={{0,8},{8,16},{16,24},{24,0},{1,9},{9,17},{17,25},{25,1},{2,10},{10... | collective-permute-start | bytes 1572872 | tf_op jit(solution)/shard_map/ppermute | solution.py:19
  43.0 0.8 copy-start.3
  43.8 14.1 %collective-permute-start.1 = (bf16[2,128,4,256]{3,0,1,2:T(2,128)(2,1)S(1)}, bf16[2,128,4,256]{3,0,1,2:T(2,128)(2,1)}, u32[]{:S(2)}, u32[]{:S(2)}) collective-permute-start(bf16[2,128,4,256]{3,0,1,2:T(2,128)(2,1)S(1)} %collective-permute-done), channel_id=1, source_target_pairs={{0,8},{8,16},{16,24},{24,0},{1,9},{9,17},{17,25},{25,1},{2,10},{10... | collective-permute-start | bytes 1572872 | tf_op jit(solution)/shard_map/ppermute | solution.py:19
  57.9 13.4 %collective-permute-start.2 = (bf16[2,128,4,256]{3,0,1,2:T(2,128)(2,1)}, bf16[2,128,4,256]{3,0,1,2:T(2,128)(2,1)}, u32[]{:S(2)}, u32[]{:S(2)}) collective-permute-start(bf16[2,128,4,256]{3,0,1,2:T(2,128)(2,1)} %collective-permute-done.1), channel_id=1, source_target_pairs={{0,8},{8,16},{16,24},{24,0},{1,9},{9,17},{17,25},{25,1},{2,10},{10... | collective-permute-start | bytes 1572872 | tf_op jit(solution)/shard_map/ppermute | solution.py:19
  100.5 0.7 copy-start.4
  100.5 0.8 copy-start.5
  100.5 0.8 copy-start.1
Sparse Core Ops, SparseCore 0:
  100.6 35.7 reduce-scatter.1
